TPU v7x, 32 devices: a whole 2x2x4 slice. The times are simulated.
32 devices in a mesh: ep: 16 (over z, y, core), rep: 2 (over x).
Axes of the slice: x: 2, y: 2, z: 4, core: 2. Of those that a mesh axis runs over, the one named last changes fastest.
Arguments:
- out_grad: bfloat16 [4096, 2048], P(('ep', 'rep')), may hold values from -6 to 6
- hidden: bfloat16 [4096, 8, 768], P(('ep', 'rep')), may hold values from -6 to 6
- expert_ids: int32 [4096, 8], P(('ep', 'rep')), may hold values from 0 to 15, all different within a row; in each aligned block of 128 rows (0 to 127, 128 to 255, ...) at most 72 rows name the same one
- gates: float32 [4096, 8], P(('ep', 'rep')), may hold values from 0.02 to 0.5
- weights: bfloat16 [16, 768, 2048], P('ep', 'rep'), may hold values from -0.125 to 0.125
- row_moment: float32 [16, 768], P('ep', 'rep'), may hold values from 16 to 1024
- col_moment: float32 [16, 2, 2048], P('ep', 'rep'), may hold values from 16 to 1024
Outputs:
- hidden_grad: bfloat16 [4096, 8, 768], P(('ep', 'rep'))
- update: bfloat16 [16, 768, 2048], P('ep', 'rep')
- row_new: float32 [16, 768], P('ep', 'rep')
- col_new: float32 [16, 2, 2048], P('ep', 'rep')
Inputs may be any that keep to these rules, and one draw needn't show every extreme that they name: `expert_ids`: the 8 experts of a token are distinct. Among the tokens of one device no expert is chosen more than 72 times, and in every draw some device reaches 72 for some expert.
All inputs are finite; a program needn't handle non-finite values.
Results may differ from a plain program's by a relative error of at most 0.014.
Values may be sent and summed in bfloat16 or wider, within the bound.
A program may use at most 128 MiB of HBM per device.

v0:
```python
import jax
import jax.numpy as jnp
from jax import lax
from jax.sharding import PartitionSpec as P

decay_rate = 0.9
epsilon = 1e-06


def local(out_grad, hidden, expert_ids, gates, weights, row_moment, col_moment):
    tok_rows, route_count = expert_ids.shape
    width = out_grad.shape[1]
    inner = hidden.shape[2]
    experts = lax.axis_size("ep")
    capacity = max(2, tok_rows * route_count * 9 // (8 * experts))
    routes = tok_rows * route_count
    flat_ids = expert_ids.reshape(routes)
    one_hot = (flat_ids[:, None] == jnp.arange(experts, dtype=jnp.int32)[None, :]).astype(jnp.int32)
    ranks = jnp.cumsum(one_hot, axis=0) - one_hot
    rank_own = jnp.sum(ranks * one_hot, axis=1)
    position = flat_ids * capacity + rank_own
    scaled = (
        (gates[:, :, None] * out_grad[:, None, :].astype(jnp.float32))
        .astype(jnp.bfloat16)
        .reshape(routes, width)
    )
    slots = experts * capacity
    send_scaled = jnp.zeros((slots, width), jnp.bfloat16).at[position].set(scaled)
    send_hidden = (
        jnp.zeros((slots, inner), jnp.bfloat16).at[position].set(hidden.reshape(routes, inner))
    )
    recv_scaled, recv_hidden = (
        lax.all_to_all(send_scaled, "ep", split_axis=0, concat_axis=0, tiled=True),
        lax.all_to_all(send_hidden, "ep", split_axis=0, concat_axis=0, tiled=True),
    )
    own_block = weights[0]
    input_grad = lax.dot_general(
        recv_scaled,
        lax.all_gather(own_block, "rep", axis=0, tiled=True),
        (((1,), (1,)), ((), ())),
        preferred_element_type=jnp.float32,
    ).astype(jnp.bfloat16)
    term = lax.dot_general(
        recv_hidden, recv_scaled, (((0,), (0,)), ((), ())), preferred_element_type=jnp.float32
    )
    gradient = lax.psum_scatter(
        lax.optimization_barrier(term.astype(jnp.bfloat16))
        .astype(jnp.float32)
        .astype(jnp.bfloat16),
        "rep",
        scatter_dimension=0,
        tiled=True,
    ).astype(jnp.float32)
    returned = lax.all_to_all(input_grad, "ep", split_axis=0, concat_axis=0, tiled=True)
    hidden_grad = returned[position].reshape(tok_rows, route_count, inner)
    squares = gradient * gradient
    row_new = decay_rate * row_moment[0] + (1.0 - decay_rate) * (
        jnp.mean(squares, axis=1) + epsilon
    )
    col_new = decay_rate * col_moment[0, 0] + (1.0 - decay_rate) * (
        jnp.mean(squares, axis=0) + epsilon
    )
    second = row_new[:, None] * col_new[None, :] / jnp.mean(row_new)
    update = (gradient * lax.rsqrt(second)).astype(jnp.bfloat16)
    return (hidden_grad, update[None], row_new[None], col_new[None, None])


def solution(mesh):
    return jax.shard_map(
        local,
        mesh=mesh,
        in_specs=(
            P(("ep", "rep"), None),
            P(("ep", "rep"), None, None),
            P(("ep", "rep"), None),
            P(("ep", "rep"), None),
            P("ep", "rep", None),
            P("ep", "rep"),
            P("ep", "rep", None),
        ),
        out_specs=(
            P(("ep", "rep"), None, None),
            P("ep", "rep", None),
            P("ep", "rep"),
            P("ep", "rep", None),
        ),
        check_vma=False,
    )
```

profile of v0, /device:TPU:15, one launch (start us, length us, event | category | flops | bytes accessed | tf_op | source)
XLA Modules:
  0.0 258.6 jit_solution(4397358027282598844)
XLA Ops:
  7.2 0.8 broadcast_multiply_fusion.1
  8.0 0.8 copy.14
  8.8 0.1 eq.29
  8.9 0.1 eq.25
  9.0 0.1 copy.13
  9.1 0.1 mul.126
  9.2 4.5 %reduce-window.6 = s32[16,8,128]{2,1,0:T(8,128)S(1)} reduce-window(s32[16,8,128]{2,1,0:T(8,128)S(1)} %fusion.17, s32[]{:T(128)} %constant.12.clone.1), window={size=1x1x128 pad=0_0x0_0x127_0}, to_apply=%region_0.0 | reduce-window | flops 2080768 | bytes 131076 | tf_op jit(solution)/shard_map/reduce-window
  13.7 0.1 slice.10
  13.8 0.1 copy.16
  13.9 0.1 copy.17
  14.0 0.1 broadcast_add_fusion
  14.2 6.6 %scatter_custom_fusion.1 = bf16[1152,768]{1,0:T(8,128)(2,1)} fusion(s32[1024]{0:T(1024)S(1)} %bitcast.55, bf16[128,8,768]{2,1,0:T(8,128)(2,1)S(1)} %copy-done, bf16[]{:T(256)} %constant.10.clone.1), kind=kCustom, calls=%fused_computation.18 | custom fusion | bytes 3342338 | tf_op jit(solution)/shard_map/scatter | solution.py:30
  20.7 6.7 %all-to-all-start.2 = ((bf16[16,72,768]{2,1,0:T(8,128)(2,1)}), bf16[16,72,768]{2,1,0:T(8,128)(2,1)}, u32[]{:S(2)}, u32[]{:S(2)}) async-start(bf16[16,72,768]{2,1,0:T(8,128)(2,1)} %bitcast.12), calls=%async_computation.2 | async-start | bytes 3538944 | tf_op jit(solution)/shard_map/all_to_all | solution.py:34
  27.4 0.1 convert_element_type.31
  27.5 0.1 copy.18
  27.6 0.1 mul.128
  27.7 9.8 %scatter_custom_fusion = bf16[1152,2048]{1,0:T(8,128)(2,1)} fusion(s32[1024]{0:T(1024)S(1)} %bitcast.56, f32[128,2048]{1,0:T(8,128)S(1)} %convert_element_type.31, f32[1024]{0:T(1024)S(1)} %mul.128, bf16[]{:T(256)} %constant.10.clone.1), kind=kCustom, calls=%fused_computation.6 | custom fusion | flops 4194304 | bytes 5771266 | tf_op jit(solution)/shard_map/scatter | solution.py:28
  37.5 30.4 %all-to-all-done.2 = bf16[16,72,768]{2,1,0:T(8,128)(2,1)} async-done(((bf16[16,72,768]{2,1,0:T(8,128)(2,1)}), bf16[16,72,768]{2,1,0:T(8,128)(2,1)}, u32[]{:S(2)}, u32[]{:S(2)}) %all-to-all-start.2) | async-done | bytes 1769504 | tf_op jit(solution)/shard_map/all_to_all | solution.py:34
  67.9 4.8 %all-to-all-start = ((bf16[16,72,2048]{2,1,0:T(8,128)(2,1)}), bf16[16,72,2048]{2,1,0:T(8,128)(2,1)}, u32[]{:S(2)}, u32[]{:S(2)}) async-start(bf16[16,72,2048]{2,1,0:T(8,128)(2,1)} %bitcast.47), calls=%async_computation | async-start | bytes 9437184 | tf_op jit(solution)/shard_map/all_to_all | solution.py:33
  72.7 0.7 all-gather.3.cloned.1.call-update
  73.4 0.2 reduce-scatter.2.cloned.1.call-start
  73.6 102.7 %all-to-all-done = bf16[16,72,2048]{2,1,0:T(8,128)(2,1)} async-done(((bf16[16,72,2048]{2,1,0:T(8,128)(2,1)}), bf16[16,72,2048]{2,1,0:T(8,128)(2,1)}, u32[]{:S(2)}, u32[]{:S(2)}) %all-to-all-start) | async-done | bytes 4718624 | tf_op jit(solution)/shard_map/all_to_all | solution.py:33
  176.4 8.8 %bitcast_convert_fusion = bf16[768,2048]{1,0:T(8,128)(2,1)} fusion(bf16[16,72,768]{2,1,0:T(8,128)(2,1)} %all-to-all-done.2, bf16[16,72,2048]{2,1,0:T(8,128)(2,1)} %all-to-all-done), kind=kOutput, calls=%fused_computation.5 | convolution fusion | flops 3625451520 | bytes 9633792 | tf_op jit(solution)/shard_map/dot_general | solution.py:43
  185.3 8.4 %convolution_convert_fusion = bf16[1152,768]{1,0:T(8,128)(2,1)} fusion(bf16[1152,2048]{1,0:T(8,128)(2,1)} %bitcast.6, bf16[1,768,2048]{2,1,0:T(8,128)(2,1)} %all-gather.3.cloned.1.call-done), kind=kOutput, calls=%fused_computation.13 | convolution fusion | flops 3624763392 | bytes 9633792 | tf_op jit(solution)/shard_map/dot_general | solution.py:37
  193.7 4.9 %all-to-all-start.1 = ((bf16[16,72,768]{2,1,0:T(8,128)(2,1)}), bf16[16,72,768]{2,1,0:T(8,128)(2,1)S(1)}, u32[]{:S(2)}, u32[]{:S(2)}) async-start(bf16[16,72,768]{2,1,0:T(8,128)(2,1)} %bitcast.48), calls=%async_computation.1 | async-start | bytes 3538944 | tf_op jit(solution)/shard_map/all_to_all | solution.py:54
  198.7 40.4 %all-to-all-done.1 = bf16[16,72,768]{2,1,0:T(8,128)(2,1)S(1)} async-done(((bf16[16,72,768]{2,1,0:T(8,128)(2,1)}), bf16[16,72,768]{2,1,0:T(8,128)(2,1)S(1)}, u32[]{:S(2)}, u32[]{:S(2)}) %all-to-all-start.1) | async-done | bytes 1769504 | tf_op jit(solution)/shard_map/all_to_all | solution.py:54
  239.0 5.2 %gather_fusion = bf16[1024,768]{1,0:T(8,128)(2,1)} fusion(bf16[1152,768]{1,0:T(8,128)(2,1)S(1)} %bitcast.46, s32[1024]{0:T(1024)S(1)} %broadcast_clamp_fusion), kind=kCustom, calls=%fused_computation | custom fusion | bytes 3149824 | tf_op jit(solution)/shard_map/gather | solution.py:55
  244.2 1.9 fusion.5
  246.1 0.6 fusion.20
  246.8 0.6 fusion.21
  247.4 0.6 reshape_add_fusion
  248.6 3.2 %fusion.10 = bf16[1,384,2048]{2,1,0:T(8,128)(2,1)} fusion(bf16[384,2048]{1,0:T(8,128)(2,1)} %reduce-scatter.2.cloned.1.call-done, f32[]{:T(128)S(6)} %div.25, f32[2048]{0:T(1024)S(1)} %fusion.19, f32[384]{0:T(512)S(1)} %get-tuple-element.7), kind=kLoop, calls=%fused_computation.17 | loop fusion | flops 3932160 | bytes 3155460 | tf_op jit(solution)/shard_map/broadcast_in_dim | solution.py:65
  (23 shorter events, 0.2 us)
Async XLA Ops:
  7.2 7.0 %copy-start = (bf16[128,8,768]{2,1,0:T(8,128)(2,1)S(1)}, bf16[128,8,768]{2,1,0:T(8,128)(2,1)}, u32[]{:S(2)}) copy-start(bf16[128,8,768]{2,1,0:T(8,128)(2,1)} %param.8) | copy-start | bytes 4718596
  14.2 13.2 %copy-start.1 = (bf16[128,2048]{1,0:T(8,128)(2,1)S(1)}, bf16[128,2048]{1,0:T(8,128)(2,1)}, u32[]{:S(2)}) copy-start(bf16[128,2048]{1,0:T(8,128)(2,1)} %param.7) | copy-start | bytes 1572868
  20.7 6.8 %copy-start.4 = (f32[128,8]{0,1:T(8,128)S(1)}, f32[128,8]{0,1:T(8,128)}, u32[]{:S(2)}) copy-start(f32[128,8]{0,1:T(8,128)} %param.10) | copy-start | bytes 12292
  20.7 47.2 %all-to-all-start.2 = ((bf16[16,72,768]{2,1,0:T(8,128)(2,1)}), bf16[16,72,768]{2,1,0:T(8,128)(2,1)}, u32[]{:S(2)}, u32[]{:S(2)}) async-start(bf16[16,72,768]{2,1,0:T(8,128)(2,1)} %bitcast.12), calls=%async_computation.2 | async-start | bytes 3538944 | tf_op jit(solution)/shard_map/all_to_all | solution.py:34
  67.9 108.5 %all-to-all-start = ((bf16[16,72,2048]{2,1,0:T(8,128)(2,1)}), bf16[16,72,2048]{2,1,0:T(8,128)(2,1)}, u32[]{:S(2)}, u32[]{:S(2)}) async-start(bf16[16,72,2048]{2,1,0:T(8,128)(2,1)} %bitcast.47), calls=%async_computation | async-start | bytes 9437184 | tf_op jit(solution)/shard_map/all_to_all | solution.py:33
  72.7 112.6 %all-gather.3.cloned.1.call-start = ((), (), s32[]{:S(2)}) async-start(), calls=%async_computation.5 | async-start | bytes 4718592 | tf_op jit(solution)/shard_map/all_gather | solution.py:39
  73.4 170.8 %reduce-scatter.2.cloned.1.call-start = ((), (), s32[]{:S(2)}) async-start(), calls=%async_computation.4 | async-start | bytes 4718592 | tf_op jit(solution)/shard_map/reduce_scatter | solution.py:46
  193.7 4.9 %copy-start.3 = (f32[1,384]{1,0:T(1,128)S(1)}, f32[1,384]{1,0:T(1,128)}, u32[]{:S(2)}) copy-start(f32[1,384]{1,0:T(1,128)} %param.12) | copy-start | bytes 4612
  193.7 45.3 %all-to-all-start.1 = ((bf16[16,72,768]{2,1,0:T(8,128)(2,1)}), bf16[16,72,768]{2,1,0:T(8,128)(2,1)S(1)}, u32[]{:S(2)}, u32[]{:S(2)}) async-start(bf16[16,72,768]{2,1,0:T(8,128)(2,1)} %bitcast.48), calls=%async_computation.1 | async-start | bytes 3538944 | tf_op jit(solution)/shard_map/all_to_all | solution.py:54
  239.0 7.1 %copy-start.2 = (f32[1,1,2048]{2,1,0:T(1,128)S(1)}, f32[1,1,2048]{2,1,0:T(1,128)}, u32[]{:S(2)}) copy-start(f32[1,1,2048]{2,1,0:T(1,128)} %param.13) | copy-start | bytes 24580
Sparse Core Ops, SparseCore 0:
  75.0 44.4 all-gather.2
  185.3 41.7 reduce-scatter.1
where the time goes:
time: 259 us
  waiting for transfers between devices  174 us (67%)
  other arithmetic  22.2 us (9%)
  matrix products  17.3 us (7%)
  starting transfers between devices  16.6 us (6%)
  between operations  14.8 us (6%)
  local copies, waits for them, and re-layouts  13.4 us (5%)
    all_to_all x1, waiting for transfers between devices, local(): lax.all_to_all(send_scaled, 'ep', split_axis=0, concat_axis=0, tiled=True)  103 us
    all_to_all x1, waiting for transfers between devices, local(): lax.all_to_all(input_grad, 'ep', split_axis=0, concat_axis=0, tiled=True)  40.4 us
    all_to_all x1, waiting for transfers between devices, local(): lax.all_to_all(send_hidden, 'ep', split_axis=0, concat_axis=0, tiled=True)  30.4 us
    scatter x1, other arithmetic, local(): jnp.zeros((slots, width), jnp.bfloat16).at[position].set(scaled)  9.76 us
    dot_general x1, matrix products, local(): lax.dot_general(recv_hidden, recv_scaled, (((0,), (0,)), ((), ())), prefe...  8.83 us
    dot_general x1, matrix products, local(): lax.dot_general(recv_scaled, lax.all_gather(own_block, 'rep', axis=0, til...  8.44 us
    all_to_all x1, starting transfers between devices, local(): lax.all_to_all(send_hidden, 'ep', split_axis=0, concat_axis=0, tiled=True)  6.65 us
    scatter x1, local copies, waits for them, and re-layouts, local(): jnp.zeros((slots, inner), jnp.bfloat16).at[position]  6.55 us
  transfers between devices with their start and end apart: 5, of which 3 were waited for; matrix products, arithmetic and copies ran while one was open for 13% of the time, Pallas kernels for 0%

commit v1 on v0

--- a/solution.py
+++ b/solution.py
@@ -5,6 +5,29 @@
 
 decay_rate = 0.9
 epsilon = 1e-06
+
+
+def in_blocks(x, dim, count):
+    shape = x.shape
+    blocks = x.reshape(*shape[:dim], count, shape[dim] // count, *shape[dim + 1 :])
+    return jnp.moveaxis(blocks, dim, 0)
+
+
+def laid_out(pieces, dim):
+    pieces = jnp.moveaxis(pieces, 0, dim)
+    shape = pieces.shape
+    return pieces.reshape(*shape[:dim], shape[dim] * shape[dim + 1], *shape[dim + 2 :])
+
+
+def rotated_exchange(value, axis, split_dim, concat_dim):
+    size, place = (lax.axis_size(axis), lax.axis_index(axis))
+    blocks = in_blocks(value, split_dim, size)
+    gathered = [blocks[place]]
+    for step in range(1, size):
+        sent = blocks[(place + step) % size]
+        gathered.append(lax.ppermute(sent, axis, [(i, (i + step) % size) for i in range(size)]))
+    blocks = jnp.stack(gathered)[(place - jnp.arange(size)) % size]
+    return laid_out(blocks, concat_dim)
 
 
 def local(out_grad, hidden, expert_ids, gates, weights, row_moment, col_moment):
@@ -30,7 +53,7 @@
         jnp.zeros((slots, inner), jnp.bfloat16).at[position].set(hidden.reshape(routes, inner))
     )
     recv_scaled, recv_hidden = (
-        lax.all_to_all(send_scaled, "ep", split_axis=0, concat_axis=0, tiled=True),
+        rotated_exchange(send_scaled, "ep", 0, 0),
         lax.all_to_all(send_hidden, "ep", split_axis=0, concat_axis=0, tiled=True),
     )
     own_block = weights[0]

time: 259 us -> 271 us (1.046)
  local copies, waits for them, and re-layouts: 13.4 us -> 40.2 us
  waiting for transfers between devices: 174 us -> 152 us
  starting transfers between devices: 16.6 us -> 23.5 us
    ppermute x0 -> x15, waiting for transfers between devices: none -> 111 us  [rotated_exchange(): lax.ppermute(sent, axis, [(i, (i + step) % size) for i in range(size)])]
    all_to_all x1 -> x0, waiting for transfers between devices: 103 us -> none  [local(): lax.all_to_all(send_scaled, 'ep', split_axis=0, concat_axis=0, tiled=True)]
    all_to_all x1, waiting for transfers between devices: 30.4 us -> 0.01 us  [local(): lax.all_to_all(send_hidden, 'ep', split_axis=0, concat_axis=0, tiled=True)]
    unnamed x12 -> x26, local copies, waits for them, and re-layouts: 0.91 us -> 16.9 us
    ppermute x0 -> x15, starting transfers between devices: none -> 12.9 us  [rotated_exchange(): lax.ppermute(sent, axis, [(i, (i + step) % size) for i in range(size)])]
    gather x0 -> x1, local copies, waits for them, and re-layouts: none -> 5.44 us  [rotated_exchange(): blocks = jnp.stack(gathered)[(place - jnp.arange(size)) % size]]
    all_to_all x1 -> x0, starting transfers between devices: 4.78 us -> none  [local(): lax.all_to_all(send_scaled, 'ep', split_axis=0, concat_axis=0, tiled=True)]
    squeeze x0 -> x1, local copies, waits for them, and re-layouts: none -> 4.48 us  [rotated_exchange(): sent = blocks[(place + step) % size]]
  transfers between devices with their start and end apart: 5 -> 19, of which waited for: 3 -> 8; matrix products, arithmetic and copies ran while one was open for 13% -> 18% of each run, Pallas kernels for 0% -> 0%
where the time goes in v1:
time: 271 us; the launch traced here: 270 us
  waiting for transfers between devices  152 us (56%)
  local copies, waits for them, and re-layouts  40.2 us (15%)
  starting transfers between devices  23.5 us (9%)
  other arithmetic  23.2 us (9%)
  matrix products  16.5 us (6%)
  between operations  15.1 us (6%)
    ppermute x15, waiting for transfers between devices, rotated_exchange(): lax.ppermute(sent, axis, [(i, (i + step) % size) for i in range(size)])  111 us
    all_to_all x1, waiting for transfers between devices, local(): lax.all_to_all(input_grad, 'ep', split_axis=0, concat_axis=0, tiled=True)  40.4 us
    unnamed x26, local copies, waits for them, and re-layouts  16.9 us
    ppermute x15, starting transfers between devices, rotated_exchange(): lax.ppermute(sent, axis, [(i, (i + step) % size) for i in range(size)])  12.9 us
    scatter x1, other arithmetic, local(): jnp.zeros((slots, width), jnp.bfloat16).at[position].set(scaled)  9.77 us
    dot_general x1, matrix products, local(): lax.dot_general(recv_scaled, lax.all_gather(own_block, 'rep', axis=0, til...  8.5 us
    dot_general x1, matrix products, local(): lax.dot_general(recv_hidden, recv_scaled, (((0,), (0,)), ((), ())), prefe...  8 us
    scatter x1, local copies, waits for them, and re-layouts, local(): jnp.zeros((slots, inner), jnp.bfloat16).at[position]  6.63 us
  transfers between devices with their start and end apart: 19, of which 8 were waited for; matrix products, arithmetic and copies ran while one was open for 18% of the time, Pallas kernels for 0%

profile of v1, /device:TPU:15, one launch (start us, length us, event | category | flops | bytes accessed | tf_op | source)
XLA Modules:
  0.0 270.2 jit_solution(902013043762925146)
XLA Ops:
  7.4 0.9 copy.14
  9.1 4.5 %reduce-window.6 = s32[16,8,128]{2,1,0:T(8,128)S(1)} reduce-window(s32[16,8,128]{2,1,0:T(8,128)S(1)} %fusion.17, s32[]{:T(128)} %constant.120.clone.1), window={size=1x1x128 pad=0_0x0_0x127_0}, to_apply=%region_0.0 | reduce-window | flops 2080768 | bytes 131076 | tf_op jit(solution)/shard_map/reduce-window
  14.3 1.1 convert_element_type.31
  16.4 9.8 %scatter_custom_fusion = bf16[1152,2048]{1,0:T(8,128)(2,1)} fusion(s32[1024]{0:T(1024)S(1)} %bitcast.118, f32[128,2048]{1,0:T(8,128)S(1)} %convert_element_type.31, f32[1024]{0:T(1024)S(1)} %mul.128, bf16[]{:T(256)} %constant.118.clone.1), kind=kCustom, calls=%fused_computation.7 | custom fusion | flops 4194304 | bytes 5771266 | tf_op jit(solution)/shard_map/scatter | solution.py:51
  26.2 4.5 %dynamic-slice_bitcast_fusion = (bf16[72,2048]{1,0:T(8,128)(2,1)}, bf16[72,2048]{1,0:T(8,128)(2,1)}, bf16[72,2048]{1,0:T(8,128)(2,1)}, bf16[72,2048]{1,0:T(8,128...) fusion(bf16[16,72,2048]{2,1,0:T(8,128)(2,1)} %bitcast.109, ...), kind=kLoop, calls=%fused_computation.37 | loop fusion | bytes 9437248 | tf_op jit(solution)/shard_map/squeeze | solution.py:27
  30.7 1.9 collective-permute-start
  32.5 1.2 collective-permute-start.1
  34.2 0.9 collective-permute-start.3
  35.1 2.7 collective-permute-start.4
  37.8 6.6 %scatter_custom_fusion.1 = bf16[1152,768]{1,0:T(8,128)(2,1)} fusion(s32[1024]{0:T(1024)S(1)} %bitcast.119, bf16[128,8,768]{2,1,0:T(8,128)(2,1)S(1)} %copy-done, bf16[]{:T(256)} %constant.118.clone.1), kind=kCustom, calls=%fused_computation.19 | custom fusion | bytes 3342338 | tf_op jit(solution)/shard_map/scatter | solution.py:53
  44.4 5.1 %all-to-all-start.1 = ((bf16[16,72,768]{2,1,0:T(8,128)(2,1)}), bf16[16,72,768]{2,1,0:T(8,128)(2,1)S(1)}, u32[]{:S(2)}, u32[]{:S(2)}) async-start(bf16[16,72,768]{2,1,0:T(8,128)(2,1)} %bitcast.43), calls=%async_computation.1 | async-start | bytes 3538944 | tf_op jit(solution)/shard_map/all_to_all | solution.py:57
  50.3 2.1 collective-permute-start.5
  52.5 1.7 bitcast_dynamic-update-slice_fusion.14
  55.0 1.7 bitcast_dynamic-update-slice_fusion.13
  56.7 2.1 collective-permute-start.7
  58.8 1.7 bitcast_dynamic-update-slice_fusion.12
  60.8 1.8 bitcast_dynamic-update-slice_fusion.11
  62.6 15.0 %collective-permute-done.4 = bf16[72,2048]{1,0:T(8,128)(2,1)} collective-permute-done((bf16[72,2048]{1,0:T(8,128)(2,1)}, bf16[72,2048]{1,0:T(8,128)(2,1)}, u32[]{:S(2)}, u32[]{:S(2)}) %collective-permute-start.4) | collective-permute-done | bytes 294944 | tf_op jit(solution)/shard_map/ppermute | solution.py:28
  77.6 1.7 bitcast_dynamic-update-slice_fusion.10
  79.3 70.3 %collective-permute-done.5 = bf16[72,2048]{1,0:T(8,128)(2,1)S(1)} collective-permute-done((bf16[72,2048]{1,0:T(8,128)(2,1)}, bf16[72,2048]{1,0:T(8,128)(2,1)S(1)}, u32[]{:S(2)}, u32[]{:S(2)}) %collective-permute-start.5) | collective-permute-done | bytes 294944 | tf_op jit(solution)/shard_map/ppermute | solution.py:28
  150.4 5.7 %collective-permute-done.6 = bf16[72,2048]{1,0:T(8,128)(2,1)S(1)} collective-permute-done((bf16[72,2048]{1,0:T(8,128)(2,1)}, bf16[72,2048]{1,0:T(8,128)(2,1)S(1)}, u32[]{:S(2)}, u32[]{:S(2)}) %collective-permute-start.6) | collective-permute-done | bytes 294944 | tf_op jit(solution)/shard_map/ppermute | solution.py:28
  156.8 11.7 %collective-permute-done.7 = bf16[72,2048]{1,0:T(8,128)(2,1)S(1)} collective-permute-done((bf16[72,2048]{1,0:T(8,128)(2,1)}, bf16[72,2048]{1,0:T(8,128)(2,1)S(1)}, u32[]{:S(2)}, u32[]{:S(2)}) %collective-permute-start.7) | collective-permute-done | bytes 294944 | tf_op jit(solution)/shard_map/ppermute | solution.py:28
  172.6 2.5 collective-permute-done.12
  175.9 4.8 %collective-permute-done.13 = bf16[72,2048]{1,0:T(8,128)(2,1)S(1)} collective-permute-done((bf16[72,2048]{1,0:T(8,128)(2,1)S(1)}, bf16[72,2048]{1,0:T(8,128)(2,1)S(1)}, u32[]{:S(2)}, u32[]{:S(2)}) %collective-permute-start.13) | collective-permute-done | bytes 294944 | tf_op jit(solution)/shard_map/ppermute | solution.py:28
  182.7 5.4 %gather_fusion = bf16[16,72,2048]{2,1,0:T(8,128)(2,1)} fusion(bf16[16,72,2048]{2,1,0:T(8,128)(2,1)} %bitcast_dynamic-update-slice_fusion, s32[1024]{0:T(1024)S(1)} %pad_clamp_fusion), kind=kCustom, calls=%fused_computation | custom fusion | bytes 9437248 | tf_op jit(solution)/shard_map/gather | solution.py:29
  188.2 8.0 %bitcast_convert_fusion = bf16[768,2048]{1,0:T(8,128)(2,1)} fusion(bf16[16,72,768]{2,1,0:T(8,128)(2,1)S(1)} %all-to-all-done.1, bf16[16,72,2048]{2,1,0:T(8,128)(2,1)} %gather_fusion), kind=kOutput, calls=%fused_computation.6 | convolution fusion | flops 3625451520 | bytes 9633792 | tf_op jit(solution)/shard_map/dot_general | solution.py:66
  196.3 8.5 %convolution_convert_fusion = bf16[1152,768]{1,0:T(8,128)(2,1)} fusion(bf16[1152,2048]{1,0:T(8,128)(2,1)} %bitcast.110, bf16[1,768,2048]{2,1,0:T(8,128)(2,1)} %all-gather.3.cloned.1.call-done), kind=kOutput, calls=%fused_computation.14 | convolution fusion | flops 3624763392 | bytes 9633792 | tf_op jit(solution)/shard_map/dot_general | solution.py:60
  204.8 5.4 %all-to-all-start = ((bf16[16,72,768]{2,1,0:T(8,128)(2,1)}), bf16[16,72,768]{2,1,0:T(8,128)(2,1)S(1)}, u32[]{:S(2)}, u32[]{:S(2)}) async-start(bf16[16,72,768]{2,1,0:T(8,128)(2,1)} %bitcast.111), calls=%async_computation | async-start | bytes 3538944 | tf_op jit(solution)/shard_map/all_to_all | solution.py:77
  210.2 40.4 %all-to-all-done = bf16[16,72,768]{2,1,0:T(8,128)(2,1)S(1)} async-done(((bf16[16,72,768]{2,1,0:T(8,128)(2,1)}), bf16[16,72,768]{2,1,0:T(8,128)(2,1)S(1)}, u32[]{:S(2)}, u32[]{:S(2)}) %all-to-all-start) | async-done | bytes 1769504 | tf_op jit(solution)/shard_map/all_to_all | solution.py:77
  250.6 5.2 %gather_fusion.1 = bf16[1024,768]{1,0:T(8,128)(2,1)} fusion(bf16[1152,768]{1,0:T(8,128)(2,1)S(1)} %bitcast.108, s32[1024]{0:T(1024)S(1)} %broadcast_clamp_fusion), kind=kCustom, calls=%fused_computation.1 | custom fusion | bytes 3149824 | tf_op jit(solution)/shard_map/gather | solution.py:78
  255.8 1.9 fusion.5
  260.1 3.2 %fusion.10 = bf16[1,384,2048]{2,1,0:T(8,128)(2,1)} fusion(bf16[384,2048]{1,0:T(8,128)(2,1)} %reduce-scatter.2.cloned.1.call-done, f32[]{:T(128)S(6)} %div.25, f32[2048]{0:T(1024)S(1)} %fusion.21, f32[384]{0:T(512)S(1)} %get-tuple-element.7), kind=kLoop, calls=%fused_computation.18 | loop fusion | flops 3932160 | bytes 3155460 | tf_op jit(solution)/shard_map/broadcast_in_dim | solution.py:88
  (70 shorter events, 15.0 us)
Async XLA Ops:
  7.2 30.6 %copy-start = (bf16[128,8,768]{2,1,0:T(8,128)(2,1)S(1)}, bf16[128,8,768]{2,1,0:T(8,128)(2,1)}, u32[]{:S(2)}) copy-start(bf16[128,8,768]{2,1,0:T(8,128)(2,1)} %param.8) | copy-start | bytes 4718596
  30.7 19.6 %collective-permute-start = (bf16[72,2048]{1,0:T(8,128)(2,1)}, bf16[72,2048]{1,0:T(8,128)(2,1)}, u32[]{:S(2)}, u32[]{:S(2)}) collective-permute-start(bf16[72,2048]{1,0:T(8,128)(2,1)} %get-tuple-element.22), channel_id=1, source_target_pairs={{0,2},{2,4},{4,6},{6,8},{8,10},{10,12},{12,14},{14,16},{16,18},{18... | collective-permute-start | bytes 884744 | tf_op jit(solution)/shard_map/ppermute | solution.py:28
  32.5 21.6 %collective-permute-start.1 = (bf16[72,2048]{1,0:T(8,128)(2,1)}, bf16[72,2048]{1,0:T(8,128)(2,1)}, u32[]{:S(2)}, u32[]{:S(2)}) collective-permute-start(bf16[72,2048]{1,0:T(8,128)(2,1)} %get-tuple-element.21), channel_id=1, source_target_pairs={{0,4},{2,6},{4,8},{6,10},{8,12},{10,14},{12,16},{14,18},{16,20},{1... | collective-permute-start | bytes 884744 | tf_op jit(solution)/shard_map/ppermute | solution.py:28
  33.8 22.9 %collective-permute-start.2 = (bf16[72,2048]{1,0:T(8,128)(2,1)}, bf16[72,2048]{1,0:T(8,128)(2,1)}, u32[]{:S(2)}, u32[]{:S(2)}) collective-permute-start(bf16[72,2048]{1,0:T(8,128)(2,1)} %get-tuple-element.20), channel_id=1, source_target_pairs={{0,6},{2,8},{4,10},{6,12},{8,14},{10,16},{12,18},{14,20},{16,22},{... | collective-permute-start | bytes 884744 | tf_op jit(solution)/shard_map/ppermute | solution.py:28
  34.2 26.3 %collective-permute-start.3 = (bf16[72,2048]{1,0:T(8,128)(2,1)}, bf16[72,2048]{1,0:T(8,128)(2,1)}, u32[]{:S(2)}, u32[]{:S(2)}) collective-permute-start(bf16[72,2048]{1,0:T(8,128)(2,1)} %get-tuple-element.19), channel_id=1, source_target_pairs={{0,8},{2,10},{4,12},{6,14},{8,16},{10,18},{12,20},{14,22},{16,24},... | collective-permute-start | bytes 884744 | tf_op jit(solution)/shard_map/ppermute | solution.py:28
  35.1 42.5 %collective-permute-start.4 = (bf16[72,2048]{1,0:T(8,128)(2,1)}, bf16[72,2048]{1,0:T(8,128)(2,1)}, u32[]{:S(2)}, u32[]{:S(2)}) collective-permute-start(bf16[72,2048]{1,0:T(8,128)(2,1)} %get-tuple-element.18), channel_id=1, source_target_pairs={{0,10},{2,12},{4,14},{6,16},{8,18},{10,20},{12,22},{14,24},{16,26}... | collective-permute-start | bytes 884744 | tf_op jit(solution)/shard_map/ppermute | solution.py:28
  44.4 143.8 %all-to-all-start.1 = ((bf16[16,72,768]{2,1,0:T(8,128)(2,1)}), bf16[16,72,768]{2,1,0:T(8,128)(2,1)S(1)}, u32[]{:S(2)}, u32[]{:S(2)}) async-start(bf16[16,72,768]{2,1,0:T(8,128)(2,1)} %bitcast.43), calls=%async_computation.1 | async-start | bytes 3538944 | tf_op jit(solution)/shard_map/all_to_all | solution.py:57
  49.5 146.7 %all-gather.3.cloned.1.call-start = ((), (), s32[]{:S(2)}) async-start(), calls=%async_computation.4 | async-start | bytes 4718592 | tf_op jit(solution)/shard_map/all_gather | solution.py:62
  50.2 205.6 %reduce-scatter.2.cloned.1.call-start = ((), (), s32[]{:S(2)}) async-start(), calls=%async_computation.3 | async-start | bytes 4718592 | tf_op jit(solution)/shard_map/reduce_scatter | solution.py:69
  50.3 118.9 %copy-start.2 = (bf16[72,2048]{1,0:T(8,128)(2,1)S(1)}, bf16[72,2048]{1,0:T(8,128)(2,1)}, u32[]{:S(2)}) copy-start(bf16[72,2048]{1,0:T(8,128)(2,1)} %get-tuple-element.9) | copy-start | bytes 884740
  50.3 119.7 %copy-start.1 = (bf16[72,2048]{1,0:T(8,128)(2,1)S(1)}, bf16[72,2048]{1,0:T(8,128)(2,1)}, u32[]{:S(2)}) copy-start(bf16[72,2048]{1,0:T(8,128)(2,1)} %get-tuple-element.8) | copy-start | bytes 884740
  50.3 99.3 %collective-permute-start.5 = (bf16[72,2048]{1,0:T(8,128)(2,1)}, bf16[72,2048]{1,0:T(8,128)(2,1)S(1)}, u32[]{:S(2)}, u32[]{:S(2)}) collective-permute-start(bf16[72,2048]{1,0:T(8,128)(2,1)} %get-tuple-element.17), channel_id=1, source_target_pairs={{0,12},{2,14},{4,16},{6,18},{8,20},{10,22},{12,24},{14,26},{16,28}... | collective-permute-start | bytes 884744 | tf_op jit(solution)/shard_map/ppermute | solution.py:28
  54.2 101.9 %collective-permute-start.6 = (bf16[72,2048]{1,0:T(8,128)(2,1)}, bf16[72,2048]{1,0:T(8,128)(2,1)S(1)}, u32[]{:S(2)}, u32[]{:S(2)}) collective-permute-start(bf16[72,2048]{1,0:T(8,128)(2,1)} %get-tuple-element.16), channel_id=1, source_target_pairs={{0,14},{2,16},{4,18},{6,20},{8,22},{10,24},{12,26},{14,28},{16,30}... | collective-permute-start | bytes 884744 | tf_op jit(solution)/shard_map/ppermute | solution.py:28
  56.7 111.8 %collective-permute-start.7 = (bf16[72,2048]{1,0:T(8,128)(2,1)}, bf16[72,2048]{1,0:T(8,128)(2,1)S(1)}, u32[]{:S(2)}, u32[]{:S(2)}) collective-permute-start(bf16[72,2048]{1,0:T(8,128)(2,1)} %get-tuple-element.15), channel_id=1, source_target_pairs={{0,16},{2,18},{4,20},{6,22},{8,24},{10,26},{12,28},{14,30},{16,0},... | collective-permute-start | bytes 884744 | tf_op jit(solution)/shard_map/ppermute | solution.py:28
  60.5 108.7 %collective-permute-start.8 = (bf16[72,2048]{1,0:T(8,128)(2,1)}, bf16[72,2048]{1,0:T(8,128)(2,1)S(1)}, u32[]{:S(2)}, u32[]{:S(2)}) collective-permute-start(bf16[72,2048]{1,0:T(8,128)(2,1)} %get-tuple-element.14), channel_id=1, source_target_pairs={{0,18},{2,20},{4,22},{6,24},{8,26},{10,28},{12,30},{14,0},{16,2},{... | collective-permute-start | bytes 884744 | tf_op jit(solution)/shard_map/ppermute | solution.py:28
  77.6 92.3 %collective-permute-start.9 = (bf16[72,2048]{1,0:T(8,128)(2,1)}, bf16[72,2048]{1,0:T(8,128)(2,1)S(1)}, u32[]{:S(2)}, u32[]{:S(2)}) collective-permute-start(bf16[72,2048]{1,0:T(8,128)(2,1)} %get-tuple-element.13), channel_id=1, source_target_pairs={{0,20},{2,22},{4,24},{6,26},{8,28},{10,30},{12,0},{14,2},{16,4},{1... | collective-permute-start | bytes 884744 | tf_op jit(solution)/shard_map/ppermute | solution.py:28
  149.6 21.5 %collective-permute-start.10 = (bf16[72,2048]{1,0:T(8,128)(2,1)}, bf16[72,2048]{1,0:T(8,128)(2,1)S(1)}, u32[]{:S(2)}, u32[]{:S(2)}) collective-permute-start(bf16[72,2048]{1,0:T(8,128)(2,1)} %get-tuple-element.12), channel_id=1, source_target_pairs={{0,22},{2,24},{4,26},{6,28},{8,30},{10,0},{12,2},{14,4},{16,6},{18... | collective-permute-start | bytes 884744 | tf_op jit(solution)/shard_map/ppermute | solution.py:28
  156.0 15.9 %collective-permute-start.11 = (bf16[72,2048]{1,0:T(8,128)(2,1)}, bf16[72,2048]{1,0:T(8,128)(2,1)S(1)}, u32[]{:S(2)}, u32[]{:S(2)}) collective-permute-start(bf16[72,2048]{1,0:T(8,128)(2,1)} %get-tuple-element.11), channel_id=1, source_target_pairs={{0,24},{2,26},{4,28},{6,30},{8,0},{10,2},{12,4},{14,6},{16,8},{18,... | collective-permute-start | bytes 884744 | tf_op jit(solution)/shard_map/ppermute | solution.py:28
  168.5 6.7 %collective-permute-start.12 = (bf16[72,2048]{1,0:T(8,128)(2,1)}, bf16[72,2048]{1,0:T(8,128)(2,1)S(1)}, u32[]{:S(2)}, u32[]{:S(2)}) collective-permute-start(bf16[72,2048]{1,0:T(8,128)(2,1)} %get-tuple-element.10), channel_id=1, source_target_pairs={{0,26},{2,28},{4,30},{6,0},{8,2},{10,4},{12,6},{14,8},{16,10},{18,... | collective-permute-start | bytes 884744 | tf_op jit(solution)/shard_map/ppermute | solution.py:28
  169.2 11.5 %collective-permute-start.13 = (bf16[72,2048]{1,0:T(8,128)(2,1)S(1)}, bf16[72,2048]{1,0:T(8,128)(2,1)S(1)}, u32[]{:S(2)}, u32[]{:S(2)}) collective-permute-start(bf16[72,2048]{1,0:T(8,128)(2,1)S(1)} %copy-done.2), channel_id=1, source_target_pairs={{0,28},{2,30},{4,0},{6,2},{8,4},{10,6},{12,8},{14,10},{16,12},{18,... | collective-permute-start | bytes 884744 | tf_op jit(solution)/shard_map/ppermute | solution.py:28
  170.0 12.0 %collective-permute-start.14 = (bf16[72,2048]{1,0:T(8,128)(2,1)S(1)}, bf16[72,2048]{1,0:T(8,128)(2,1)S(1)}, u32[]{:S(2)}, u32[]{:S(2)}) collective-permute-start(bf16[72,2048]{1,0:T(8,128)(2,1)S(1)} %copy-done.1), channel_id=1, source_target_pairs={{0,30},{2,0},{4,2},{6,4},{8,6},{10,8},{12,10},{14,12},{16,14},{18,... | collective-permute-start | bytes 884744 | tf_op jit(solution)/shard_map/ppermute | solution.py:28
  196.2 13.9 %copy-start.4 = (f32[1,384]{1,0:T(1,128)S(1)}, f32[1,384]{1,0:T(1,128)}, u32[]{:S(2)}) copy-start(f32[1,384]{1,0:T(1,128)} %param.12) | copy-start | bytes 4612
  204.8 45.8 %all-to-all-start = ((bf16[16,72,768]{2,1,0:T(8,128)(2,1)}), bf16[16,72,768]{2,1,0:T(8,128)(2,1)S(1)}, u32[]{:S(2)}, u32[]{:S(2)}) async-start(bf16[16,72,768]{2,1,0:T(8,128)(2,1)} %bitcast.111), calls=%async_computation | async-start | bytes 3538944 | tf_op jit(solution)/shard_map/all_to_all | solution.py:77
  250.6 7.1 %copy-start.3 = (f32[1,1,2048]{2,1,0:T(1,128)S(1)}, f32[1,1,2048]{2,1,0:T(1,128)}, u32[]{:S(2)}) copy-start(f32[1,1,2048]{2,1,0:T(1,128)} %param.13) | copy-start | bytes 24580
Sparse Core Ops, SparseCore 0:
  51.8 44.4 all-gather.2
  196.3 42.3 reduce-scatter.1
